TPU v7x, 32 devices: a whole 2x2x4 slice. The times are simulated.
32 devices in a mesh: sec: 2 (over core), req: 4 (over z), head: 4 (over y, x).
Axes of the slice: x: 2, y: 2, z: 4, core: 2. Of those that a mesh axis runs over, the one named last changes fastest.
Arguments:
- queries: bfloat16 [32, 32, 4096], P(('sec', 'req'), None, 'head'), as said below
- tree_keys: bfloat16 [32, 32, 512], P(('sec', 'req'), None, 'head'), may hold values from -4 to 4
- tree_values: bfloat16 [32, 32, 512], P(('sec', 'req'), None, 'head'), may hold values from -4 to 4
- cache_keys: bfloat16 [32, 4, 4096, 128], P(('sec', 'req'), 'head'), as said below
- cache_values: bfloat16 [32, 4, 4096, 128], P(('sec', 'req'), 'head'), may hold values from -4 to 4
- cache_lengths: int32 [32], P(('sec', 'req')), may hold values from 1024 to 4096
- tree_parents: int32 [32, 32], P(('sec', 'req')), may hold values from 0 to 30, as said below
- out_weight: bfloat16 [4096, 2048], P('head'), may hold values from -0.09375 to 0.09375
- hidden: bfloat16 [1024, 2048], P(('sec', 'req', 'head')), may hold values from -0.1796875 to 0.1796875
- norm_gain: float32 [2048], replicated, may hold values from 0.1 to 1.9
- expert_ids: int32 [1024, 8], P(('sec', 'req', 'head')), may hold values from 0 to 31, all different within a row; in each aligned block of 32 rows (0 to 31, 32 to 63, ...) at most 16 rows name the same one
- route_weights: float32 [1024, 8], P(('sec', 'req', 'head')), may hold values from 0.05 to 0.25
- expert_gate_up: bfloat16 [32, 2048, 1536], P(('sec', 'req', 'head')), may hold values from -0.125 to 0.125
- expert_down: bfloat16 [32, 768, 2048], P(('sec', 'req', 'head')), may hold values from -0.21875 to 0.21875
Outputs:
- layer_out: bfloat16 [1024, 2048], P(('sec', 'req', 'head'))
Inputs may be any that keep to these rules, and one draw needn't show every extreme that they name: `queries`: values lie within -4.5 to 4.5. `cache_keys`: values lie within -4.5 to 4.5. tree_parents[r, i] < i for i >= 1, and tree_parents[r, 0] = 0. `expert_ids`: each row names 8 different experts. Among the 32 rows of one device (aligned blocks of rows), no expert is named more than 16 times, a bound that some block reaches.
All inputs are finite; a program needn't handle non-finite values.
Results may differ from a plain program's by a relative error of at most 0.02.
Values may be sent and summed in bfloat16 or wider, within the bound.
A program may use at most 128 MiB of HBM per device.

v0:
```python
import functools
import math

import jax
import jax.numpy as jnp
from jax import lax
from jax.experimental import pallas as pl
from jax.experimental.pallas import tpu as pltpu
from jax.sharding import PartitionSpec as P

F32 = jnp.float32
BF16 = jnp.bfloat16
NEG = -1e30
CHUNKS = (2048, 512)
LANES = 128


def dot_nt(a, b):
    return lax.dot_general(a, b, (((1,), (1,)), ((), ())), preferred_element_type=F32)


def dot_nn(a, b):
    return jnp.dot(a, b, preferred_element_type=F32)


def attend_kernel(
    len_ref, q_ref, tk_ref, tv_ref, par_ref, ck_ref, cv_ref, wo_hbm, out_ref,
    attended, m_ref, l_ref, acc_ref, wo_ref, wo_sem,
):
    r = pl.program_id(0)
    last = pl.num_programs(0) - 1
    weights = pltpu.make_async_copy(wo_hbm, wo_ref, wo_sem)

    @pl.when(r == 0)
    def _():
        weights.start()

    tree, width = q_ref.shape[1:]
    hd = ck_ref.shape[3]
    cache = ck_ref.shape[2]
    groups = width // hd
    scale = hd ** (-0.5) * math.log2(math.e)
    q = q_ref[0]
    rows = jnp.concatenate([q[:, g * hd : (g + 1) * hd] for g in range(groups)], axis=0)

    down = lax.broadcasted_iota(jnp.int32, (tree, tree), 0)
    across = lax.broadcasted_iota(jnp.int32, (tree, tree), 1)
    eye = (down == across).astype(F32)
    linked_t = (jnp.broadcast_to(par_ref[0], (tree, tree)) == down).astype(F32)
    closure = jnp.minimum(dot_nt(eye.astype(BF16), linked_t.astype(BF16)) + eye, 1.0)
    for _ in range(max(1, (tree - 1).bit_length())):
        half = closure.astype(BF16)
        closure = jnp.minimum(dot_nn(half, half), 1.0)
    admitted = jnp.concatenate([closure] * groups, axis=0)

    scores = jnp.where(admitted > 0.5, dot_nt(rows, tk_ref[0]) * scale, NEG)
    highest = jnp.max(scores, -1, keepdims=True)
    probs = jnp.exp2(scores - highest)
    m_ref[...] = jnp.broadcast_to(highest, m_ref.shape)
    l_ref[...] = jnp.broadcast_to(jnp.sum(probs, -1, keepdims=True), l_ref.shape)
    acc_ref[...] = dot_nn(probs.astype(BF16), tv_ref[0])

    length = len_ref[r]

    def step(start, chunk, masked):
        start = pl.multiple_of(start, chunk)
        s = dot_nt(rows, ck_ref[0, 0, pl.ds(start, chunk), :]) * scale
        if masked:
            place = lax.broadcasted_iota(jnp.int32, s.shape, 1)
            s = jnp.where(place < length - start, s, NEG)
        before = m_ref[:, :1]
        now = jnp.maximum(before, jnp.max(s, -1, keepdims=True))
        p = jnp.exp2(s - now)
        fade = jnp.exp2(before - now)
        l_ref[...] = l_ref[...] * fade + jnp.sum(p, -1, keepdims=True)
        acc_ref[...] = acc_ref[...] * fade + dot_nn(
            p.astype(BF16), cv_ref[0, 0, pl.ds(start, chunk), :]
        )
        m_ref[...] = jnp.broadcast_to(now, m_ref.shape)

    done = 0
    for chunk in CHUNKS:
        assert cache % chunk == 0
        upto = length // chunk

        @pl.loop(done // chunk, upto)
        def _(i, chunk=chunk):
            step(i * chunk, chunk, False)

        done = upto * chunk

    @pl.when(done < length)
    def _():
        step(done, CHUNKS[-1], True)

    o = (acc_ref[...] / l_ref[:, :1]).astype(BF16)
    for g in range(groups):
        attended[r, :, g * hd : (g + 1) * hd] = o[g * tree : (g + 1) * tree]

    @pl.when(r == last)
    def _():
        weights.wait()
        a = attended[...].reshape(-1, width)
        out_ref[...] = dot_nn(a, wo_ref[...]).astype(BF16)


def attend(queries, tree_keys, tree_values, cache_keys, cache_values, lengths, parents, out_weight):
    req, tree, width = queries.shape
    cache, hd = cache_keys.shape[2:]
    assert cache_keys.shape[1] == 1
    model = out_weight.shape[1]
    rows = tree * (width // hd)
    grid_spec = pltpu.PrefetchScalarGridSpec(
        num_scalar_prefetch=1,
        grid=(req,),
        in_specs=[
            pl.BlockSpec((1, tree, width), lambda r, n: (r, 0, 0)),
            pl.BlockSpec((1, tree, hd), lambda r, n: (r, 0, 0)),
            pl.BlockSpec((1, tree, hd), lambda r, n: (r, 0, 0)),
            pl.BlockSpec((1, 1, tree), lambda r, n: (r, 0, 0)),
            pl.BlockSpec((1, 1, cache, hd), lambda r, n: (r, 0, 0, 0)),
            pl.BlockSpec((1, 1, cache, hd), lambda r, n: (r, 0, 0, 0)),
            pl.BlockSpec(memory_space=pl.ANY),
        ],
        out_specs=pl.BlockSpec((req * tree, model), lambda r, n: (0, 0)),
        scratch_shapes=[
            pltpu.VMEM((req, tree, width), BF16),
            pltpu.VMEM((rows, LANES), F32),
            pltpu.VMEM((rows, LANES), F32),
            pltpu.VMEM((rows, hd), F32),
            pltpu.VMEM(out_weight.shape, BF16),
            pltpu.SemaphoreType.DMA,
        ],
    )
    return pl.pallas_call(
        attend_kernel,
        grid_spec=grid_spec,
        out_shape=jax.ShapeDtypeStruct((req * tree, model), BF16),
        compiler_params=pltpu.CompilerParams(
            dimension_semantics=("arbitrary",), vmem_limit_bytes=67043328
        ),
    )(lengths, queries, tree_keys, tree_values, parents.reshape(req, 1, tree), cache_keys,
      cache_values, out_weight)


def copy_count(z_n, y_n, x_n):
    gather = 2 * (z_n - 1) + z_n * (x_n * y_n - 1) * 2 + 2 * z_n * y_n * x_n
    back = 2 * z_n + 2 * z_n * (y_n - 1 + x_n - 1) + 2 * (z_n - 1)
    return (y_n * x_n - 1) + gather + back


def expert_kernel(
    dims, part_ref, hid_ref, gain_ref, ids_ref, rw_ref, gu_hbm, dn_hbm, out_ref,
    head_in, bank, sums, pair_in, first_in, second_in, z_in, resid_ref, gu, dn,
    send, recv, load_sem,
):
    z_n, y_n, x_n = dims
    h_n = y_n * x_n
    s = lax.axis_index("sec")
    z = lax.axis_index("req")
    h = lax.axis_index("head")
    y = h // x_n
    x = h % x_n
    tok, model = hid_ref.shape
    half = model // 2
    mine = (s * z_n + z) * h_n + h

    def to_head(k):
        return {"head": lax.rem(h + k, h_n)}

    def to_z(k):
        return {"req": lax.rem(z + k, z_n)}

    def to_yx(dy, dx):
        return {"head": lax.rem(y + dy, y_n) * x_n + lax.rem(x + dx, x_n)}

    partner = {"sec": 1 - s}
    barrier = pltpu.get_barrier_semaphore()
    peers = [to_head(k) for k in range(1, h_n)] + [to_z(k) for k in range(1, z_n)] + [partner]
    for peer in peers:
        pl.semaphore_signal(
            barrier, inc=1, device_id=peer, device_id_type=pl.DeviceIdType.MESH
        )
    load_gu = pltpu.make_async_copy(gu_hbm.at[0], gu, load_sem.at[0])
    load_dn = pltpu.make_async_copy(dn_hbm.at[0], dn, load_sem.at[1])
    load_gu.start()
    load_dn.start()
    pl.semaphore_wait(barrier, len(peers))

    made = []

    def push(src, dst, peer):
        k = len(made)
        c = pltpu.make_async_remote_copy(
            src_ref=src, dst_ref=dst, send_sem=send.at[k], recv_sem=recv.at[k],
            device_id=peer, device_id_type=pl.DeviceIdType.MESH,
        )
        made.append(c)
        c.start()
        return c

    arrivals = []
    for k in range(1, h_n):
        row = pl.multiple_of(lax.rem(h + k, h_n) * tok, tok)
        arrivals.append(push(part_ref.at[pl.ds(row, tok), :], head_in.at[k - 1], to_head(k)))
    lanes = bank.shape[-1] - half
    labels = lax.broadcasted_iota(jnp.int32, (lanes, tok), 0)
    dense = jnp.zeros((lanes, tok), F32)
    for k in range(ids_ref.shape[0]):
        dense = dense + jnp.where(ids_ref[k : k + 1, :] == labels, rw_ref[k : k + 1, :], 0.0)
    high = dense.astype(BF16)
    low = (dense - high.astype(F32)).astype(BF16)
    eye = (
        lax.broadcasted_iota(jnp.int32, (tok, tok), 0)
        == lax.broadcasted_iota(jnp.int32, (tok, tok), 1)
    ).astype(F32).astype(BF16)
    high = dot_nt(eye, high).astype(BF16)
    low = dot_nt(eye, low).astype(BF16)
    own_row = pl.multiple_of(h * tok, tok)
    resid = hid_ref[...].astype(F32) + part_ref[pl.ds(own_row, tok), :].astype(F32)
    for k in range(1, h_n):
        arrivals[k - 1].wait_recv()
        resid = resid + head_in[k - 1].astype(F32)
    resid_ref[...] = resid
    normed = (
        resid * lax.rsqrt(jnp.mean(resid * resid, -1, keepdims=True) + 1e-06) * gain_ref[...]
    ).astype(BF16)
    for f, extra in ((0, high), (1, low)):
        bank[0, f, 0, 0, 0, :, :half] = normed[:, f * half : (f + 1) * half]
        bank[0, f, 0, 0, 0, :, half:] = extra

    got = {}

    def gather(f, dz, dy, dx, src, peer):
        got[f, dz, dy, dx] = push(
            bank.at[(0, f, dz) + src], bank.at[0, f, dz, dy, dx], peer
        )

    for dz in range(1, z_n):
        for f in range(2):
            got[f, dz, 0, 0] = push(bank.at[0, f, 0, 0, 0], bank.at[0, f, dz, 0, 0], to_z(dz))

    crossed = {}

    def cross(f, dz, dy, dx):
        crossed[f, dz, dy, dx] = push(
            bank.at[0, f, dz, dy, dx], bank.at[1, f, dz, dy, dx], partner
        )

    def stage_a(dz):
        for f in range(2):
            if dz:
                got[f, dz, 0, 0].wait_recv()
            cross(f, dz, 0, 0)
            for dx in range(1, x_n):
                gather(f, dz, 0, dx, (0, 0), to_yx(0, dx)) if f == 0 else None
            for dy in range(1, y_n):
                gather(f, dz, dy, 0, (0, 0), to_yx(dy, 0)) if f == 1 else None
        for dy in range(1, y_n):
            gather(0, dz, dy, 0, (0, 0), to_yx(dy, 0))
        for dx in range(1, x_n):
            gather(1, dz, 0, dx, (0, 0), to_yx(0, dx))

    def stage_b(dz):
        for dx in range(1, x_n):
            got[0, dz, 0, dx].wait_recv()
            for dy in range(1, y_n):
                gather(0, dz, dy, dx, (0, dx), to_yx(dy, 0))
            cross(0, dz, 0, dx)
        for dy in range(1, y_n):
            got[1, dz, dy, 0].wait_recv()
            for dx in range(1, x_n):
                gather(1, dz, dy, dx, (dy, 0), to_yx(0, dx))
            cross(1, dz, dy, 0)

    def stage_c(dz):
        for f in range(2):
            for dy in range(y_n):
                for dx in range(x_n):
                    seen = (dy == 0 and dx == 0) or (f == 0 and dy == 0) or (f == 1 and dx == 0)
                    if not seen:
                        got[f, dz, dy, dx].wait_recv()
                        cross(f, dz, dy, dx)

    count = 2 * h_n * tok
    apart = 1 if h_n * tok <= 128 else y_n

    def experts(dz):
        for f in range(2):
            for dy in range(y_n):
                for dx in range(x_n):
                    crossed[f, dz, dy, dx].wait_recv()
        pick = lax.broadcasted_iota(jnp.int32, (1, lanes), 1) == mine
        for part in range(apart):
            ys = slice(part * (y_n // apart), (part + 1) * (y_n // apart))
            left = bank[:, 0, dz, ys].reshape(count // apart, half + lanes)
            right = bank[:, 1, dz, ys].reshape(count // apart, half + lanes)
            named = left[:, half:].astype(F32) + right[:, half:].astype(F32)
            weight = jnp.sum(jnp.where(pick, named, 0.0), -1, keepdims=True)
            mixed = dot_nn(left[:, :half], gu[:half]) + dot_nn(right[:, :half], gu[half:])
            hidden = mixed.shape[1] // 2
            gate = mixed[:, :hidden]
            active = (gate / (1.0 + jnp.exp(-gate)) * mixed[:, hidden:]).astype(BF16)
            result = jnp.where(weight > 0.0, dot_nn(active, dn[...]) * weight, 0.0).astype(BF16)
            shaped = result.reshape(2, y_n // apart, x_n, tok, model)
            for f in range(2):
                sums[f, dz, ys] = shaped[0, ..., f * half : (f + 1) * half]
                bank[1, f, dz, ys, :, :, :half] = shaped[1, ..., f * half : (f + 1) * half]

    paired, firsts, seconds, ends = {}, {}, {}, {}

    def back_pair(dz):
        for f in range(2):
            paired[f, dz] = push(
                bank.at[1, f, dz, :, :, :, pl.ds(0, half)], pair_in.at[f, dz], partner
            )

    def back_first(dz):
        for f in range(2):
            paired[f, dz].wait_recv()
            sums[f, dz] = (sums[f, dz].astype(F32) + pair_in[f, dz].astype(F32)).astype(BF16)
            if f == 0:
                for dy in range(1, y_n):
                    firsts[f, dz, dy] = push(
                        sums.at[f, dz, dy], first_in.at[f, dz, dy - 1], to_yx(y_n - dy, 0)
                    )
            else:
                for dx in range(1, x_n):
                    firsts[f, dz, dx] = push(
                        sums.at[f, dz, :, dx], first_in.at[f, dz, dx - 1], to_yx(0, x_n - dx)
                    )

    def back_second(dz):
        for f in range(2):
            total = sums[f, dz, 0] if f == 0 else sums[f, dz, :, 0]
            total = total.astype(F32)
            for d in range(1, y_n if f == 0 else x_n):
                firsts[f, dz, d].wait_recv()
                total = total + first_in[f, dz, d - 1].astype(F32)
            if f == 0:
                sums[f, dz, 0] = total.astype(BF16)
                for dx in range(1, x_n):
                    seconds[f, dz, dx] = push(
                        sums.at[f, dz, 0, dx], second_in.at[f, dz, dx - 1], to_yx(0, x_n - dx)
                    )
            else:
                sums[f, dz, :, 0] = total.astype(BF16)
                for dy in range(1, y_n):
                    seconds[f, dz, dy] = push(
                        sums.at[f, dz, dy, 0], second_in.at[f, dz, dy - 1], to_yx(y_n - dy, 0)
                    )

    def back_end(dz):
        for f in range(2):
            total = sums[f, dz, 0, 0].astype(F32)
            for d in range(1, x_n if f == 0 else y_n):
                seconds[f, dz, d].wait_recv()
                total = total + second_in[f, dz, d - 1].astype(F32)
            if dz:
                sums[f, dz, 0, 0] = total.astype(BF16)
                ends[f, dz] = push(sums.at[f, dz, 0, 0], z_in.at[f, dz - 1], to_z(z_n - dz))
            else:
                cols = slice(f * half, (f + 1) * half)
                resid_ref[:, cols] = resid_ref[:, cols] + total

    order = list(range(1, z_n)) + [0]

    def back(j):
        for stage, lag in ((back_end, 3), (back_second, 2), (back_first, 1)):
            if 0 <= j - lag < z_n:
                stage(order[j - lag])

    ran = 0
    for i in range(z_n + 2):
        for stage, lag in ((stage_a, 0), (stage_b, 1), (stage_c, 2)):
            if 0 <= i - lag < z_n:
                stage(i - lag)
        if i == 2:
            load_gu.wait()
            load_dn.wait()
        while ran < z_n and (i == z_n + 1 or order[ran] <= i - 2 and order[ran] > 0):
            experts(order[ran])
            back_pair(order[ran])
            back(ran)
            ran += 1
    for j in range(z_n, z_n + 3):
        back(j)
    for f in range(2):
        cols = slice(f * half, (f + 1) * half)
        total = resid_ref[:, cols]
        for dz in range(1, z_n):
            ends[f, dz].wait_recv()
            total = total + z_in[f, dz - 1].astype(F32)
        out_ref[:, cols] = total.astype(BF16)
    for c in made:
        c.wait_send()
    assert len(made) == copy_count(*dims)


def expert_layer(dims, partial, hidden, gain, ids, route, gate_up, down):
    z_n, y_n, x_n = dims
    tok, model = hidden.shape
    half = model // 2
    experts = gate_up.shape[0] * 2 * z_n * y_n * x_n
    assert gate_up.shape[0] == 1 and partial.shape[0] == y_n * x_n * tok
    lanes = -(-experts // LANES) * LANES
    most = max(y_n, x_n)
    copies = copy_count(*dims)
    vmem = pl.BlockSpec(memory_space=pltpu.VMEM)
    return pl.pallas_call(
        functools.partial(expert_kernel, dims),
        out_shape=jax.ShapeDtypeStruct((tok, model), BF16),
        in_specs=[vmem] * 5 + [pl.BlockSpec(memory_space=pl.ANY)] * 2,
        out_specs=vmem,
        scratch_shapes=[
            pltpu.VMEM((y_n * x_n - 1, tok, model), BF16),
            pltpu.VMEM((2, 2, z_n, y_n, x_n, tok, half + lanes), BF16),
            pltpu.VMEM((2, z_n, y_n, x_n, tok, half), BF16),
            pltpu.VMEM((2, z_n, y_n, x_n, tok, half), BF16),
            pltpu.VMEM((2, z_n, most - 1, most, tok, half), BF16),
            pltpu.VMEM((2, z_n, most - 1, tok, half), BF16),
            pltpu.VMEM((2, z_n - 1, tok, half), BF16),
            pltpu.VMEM((tok, model), F32),
            pltpu.VMEM(gate_up.shape[1:], BF16),
            pltpu.VMEM(down.shape[1:], BF16),
            pltpu.SemaphoreType.DMA((copies,)),
            pltpu.SemaphoreType.DMA((copies,)),
            pltpu.SemaphoreType.DMA((2,)),
        ],
        compiler_params=pltpu.CompilerParams(
            collective_id=0, has_side_effects=True, vmem_limit_bytes=67043328
        ),
    )(partial, hidden, gain.reshape(1, -1), ids.T, route.T, gate_up, down)


def per_device(
    dims, queries, tree_keys, tree_values, cache_keys, cache_values, cache_lengths, tree_parents,
    out_weight, hidden, norm_gain, expert_ids, route_weights, expert_gate_up, expert_down,
):
    partial = attend(
        queries, tree_keys, tree_values, cache_keys, cache_values, cache_lengths, tree_parents,
        out_weight,
    )
    return expert_layer(
        dims, partial, hidden, norm_gain, expert_ids, route_weights, expert_gate_up, expert_down
    )


def solution(mesh):
    heads = mesh.shape["head"]
    x_n = math.isqrt(heads)
    while heads % x_n:
        x_n -= 1
    assert mesh.shape["sec"] == 2
    dims = (mesh.shape["req"], heads // x_n, x_n)
    tokens = ("sec", "req", "head")
    in_specs = (
        P(("sec", "req"), None, "head"),
        P(("sec", "req"), None, "head"),
        P(("sec", "req"), None, "head"),
        P(("sec", "req"), "head", None, None),
        P(("sec", "req"), "head", None, None),
        P(("sec", "req")),
        P(("sec", "req"), None),
        P("head", None),
        P(tokens, None),
        P(),
        P(tokens, None),
        P(tokens, None),
        P(tokens, None, None),
        P(tokens, None, None),
    )
    return jax.shard_map(
        functools.partial(per_device, dims), mesh=mesh, in_specs=in_specs,
        out_specs=P(tokens, None), check_vma=False,
    )
```

profile of v0, /device:TPU:0, one launch (start us, length us, event | category | flops | bytes accessed | tf_op | source)
XLA Modules:
  0.0 91.9 jit_solution(3254530599383489505)
XLA Ops:
  0.0 18.1 %shard_map.136.part_ref = bf16[128,2048]{1,0:T(8,128)(2,1)} custom-call(s32[4]{0:T(128)} %len_ref.1, bf16[4,32,1024]{2,1,0:T(8,128)(2,1)} %q_ref.1, bf16[4,32,128]{2,1,0:T(8,128)(2,1)} %tk_ref.1, bf16[4,32,128]{2,1,0:T(8,128)(2,1)} %tv_ref.1, s32[4,1,32]{2,1,0:T(1,128)} %bitcast.9, bf16[4,1,4096,128]{3,2,1,0:T(8,128)(2,1)} %ck_ref.1, ...), custom_call_target="tpu_custom_call" | custom-call | tf_op jit(solution)/shard_map/pallas_call | solution.py:135
  18.1 72.3 %shard_map.137 = bf16[32,2048]{1,0:T(8,128)(2,1)} custom-call(bf16[128,2048]{1,0:T(8,128)(2,1)} %shard_map.136.part_ref, bf16[32,2048]{1,0:T(8,128)(2,1)} %hid_ref.1, f32[1,2048]{1,0:T(1,128)} %bitcast.6, s32[8,32]{1,0:T(8,128)} %bitcast.7, f32[8,32]{1,0:T(8,128)} %bitcast.8, bf16[1,2048,1536]{2,1,0:T(8,128)(2,1)} %gu_hbm.1, bf16[1,768,2048]{2,1,0:T(8,128)(2,1)} %dn_hbm.1), custom_call_target="tpu_custom_call" | custom-call | tf_op jit(solution)/shard_map/pallas_call | solution.py:410
  90.3 1.6 %copy.17 = bf16[32,2048]{1,0:T(8,128)(2,1)} copy(bf16[32,2048]{1,0:T(8,128)(2,1)} %shard_map.137) | data formatting | bytes 262144
where the time goes:
time: 92.1 us; the launch traced here: 91.9 us
  Pallas kernels  90.3 us (98%)
  local copies, waits for them, and re-layouts  1.57 us (2%)
    pallas_call x1, Pallas kernels, expert_layer(): pl.pallas_call(functools.partial(expert_kernel, dims), out_shape=jax.Shap...  72.3 us
    pallas_call x1, Pallas kernels, attend(): pl.pallas_call(attend_kernel, grid_spec=grid_spec, out_shape=jax.ShapeDty...  18.1 us

commit v1 on v0

v1 whole, which is shorter than its diff:
```python
import functools
import math

import jax
import jax.numpy as jnp
from jax import lax
from jax.experimental import pallas as pl
from jax.experimental.pallas import tpu as pltpu
from jax.sharding import PartitionSpec as P

F32 = jnp.float32
BF16 = jnp.bfloat16
NEG = -1e30
CHUNK = 2048
LANES = 128


def dot_nt(a, b):
    return lax.dot_general(a, b, (((1,), (1,)), ((), ())), preferred_element_type=F32)


def dot_nn(a, b):
    return jnp.dot(a, b, preferred_element_type=F32)


def copy_count(z_n, y_n, x_n):
    gather = 2 * (z_n - 1) + z_n * (x_n * y_n - 1) * 2 + 2 * z_n * y_n * x_n
    back = 2 * z_n + 2 * z_n * (y_n - 1 + x_n - 1) + 2 * (z_n - 1)
    route = (z_n - 1) + (y_n * x_n - 1) + 1
    return (y_n * x_n - 1) + gather + back + route


def closures(par_ref):
    n, tree = par_ref.shape
    down = lax.broadcasted_iota(jnp.int32, (tree, tree), 0)
    across = lax.broadcasted_iota(jnp.int32, (tree, tree), 1)
    eye = (down == across).astype(F32)
    result = []
    for r in range(n):
        linked_t = (jnp.broadcast_to(par_ref[r : r + 1, :], (tree, tree)) == down).astype(F32)
        linked = dot_nt(eye.astype(BF16), linked_t.astype(BF16))
        result.append(jnp.minimum(linked + eye, 1.0))
    for _ in range(max(1, (tree - 1).bit_length())):
        result = [jnp.minimum(dot_nn(c.astype(BF16), c.astype(BF16)), 1.0) for c in result]
    return result


def layer_kernel(
    dims, len_ref, q_ref, tk_ref, tv_ref, par_ref, hid_ref, gain_ref, ids_ref, rw_ref,
    ck_hbm, cv_hbm, wo_hbm, gu_hbm, dn_hbm, out_ref,
    kbuf, vbuf, wide, closed, attended, part_out, head_in, routes,
    bank, sums, pair_in, first_in, second_in, z_in, resid_ref, gu,
    send, recv, load_sem, kv_sem,
):
    z_n, y_n, x_n = dims
    h_n = y_n * x_n
    s = lax.axis_index("sec")
    z = lax.axis_index("req")
    h = lax.axis_index("head")
    y = h // x_n
    x = h % x_n
    tok, model = hid_ref.shape
    half = model // 2
    mine = (s * z_n + z) * h_n + h

    def to_head(k):
        return {"head": lax.rem(h + k, h_n)}

    def to_z(k):
        return {"req": lax.rem(z + k, z_n)}

    def to_yx(dy, dx):
        return {"head": lax.rem(y + dy, y_n) * x_n + lax.rem(x + dx, x_n)}

    partner = {"sec": 1 - s}
    barrier = pltpu.get_barrier_semaphore()
    peers = [to_head(k) for k in range(1, h_n)] + [to_z(k) for k in range(1, z_n)] + [partner]
    for peer in peers:
        pl.semaphore_signal(
            barrier, inc=1, device_id=peer, device_id_type=pl.DeviceIdType.MESH
        )

    reqs, tree, width = q_ref.shape
    assert reqs == h_n and tree == tok
    which = [lax.rem(h + k, h_n) for k in range(1, h_n + 1)]
    load_k = [
        pltpu.make_async_copy(ck_hbm.at[which[k], 0], kbuf.at[k % 2], kv_sem.at[0, k])
        for k in range(reqs)
    ]
    load_v = [
        pltpu.make_async_copy(cv_hbm.at[which[k], 0], vbuf.at[k % 2], kv_sem.at[1, k])
        for k in range(reqs)
    ]
    load_wo = pltpu.make_async_copy(wo_hbm, wide.at[pl.ds(0, width)], load_sem.at[2])
    load_gu = pltpu.make_async_copy(gu_hbm.at[0], gu, load_sem.at[0])
    ffe = dn_hbm.shape[1]
    load_dn = pltpu.make_async_copy(dn_hbm.at[0], wide.at[pl.ds(0, ffe)], load_sem.at[1])
    for k in range(2):
        load_k[k].start()
        load_v[k].start()
    load_wo.start()
    load_gu.start()

    made = []

    def push(src, dst, peer):
        k = len(made)
        c = pltpu.make_async_remote_copy(
            src_ref=src, dst_ref=dst, send_sem=send.at[k], recv_sem=recv.at[k],
            device_id=peer, device_id_type=pl.DeviceIdType.MESH,
        )
        made.append(c)
        c.start()
        return c

    lanes = routes.shape[-1]
    labels = lax.broadcasted_iota(jnp.int32, (lanes, tok), 0)
    dense = jnp.zeros((lanes, tok), F32)
    for k in range(ids_ref.shape[0]):
        dense = dense + jnp.where(ids_ref[k : k + 1, :] == labels, rw_ref[k : k + 1, :], 0.0)
    routes[0, 0, 0] = dense.T

    for r, c in enumerate(closures(par_ref)):
        closed[r] = c

    cache, hd = ck_hbm.shape[2:]
    groups = width // hd
    scale = hd ** (-0.5) * math.log2(math.e)
    chunks = cache // CHUNK
    assert cache % CHUNK == 0
    state = {}

    def rows_of(k):
        q = q_ref[which[k]]
        rows = jnp.concatenate([q[:, g * hd : (g + 1) * hd] for g in range(groups)], axis=0)
        return (rows.astype(F32) * scale).astype(BF16)

    def score(k, c):
        if c == 0:
            state[k] = rows_of(k)
        sc = dot_nt(state[k], kbuf[k % 2, c * CHUNK : (c + 1) * CHUNK])
        place = lax.broadcasted_iota(jnp.int32, (1, CHUNK), 1)
        return sc + jnp.where(place < len_ref[which[k]] - c * CHUNK, 0.0, NEG)

    def project(ks):
        a = attended[ks[0] : ks[-1] + 1].reshape(len(ks) * tree, width)
        return dot_nn(a, wide[:width])

    arrivals = []

    def send_part(ks):
        out = project(ks).astype(BF16)
        for i, k in enumerate(ks):
            part_out[k] = out[i * tok : (i + 1) * tok]
        for k in ks:
            arrivals.append(push(part_out.at[k], head_in.at[k], to_head(k + 1)))

    route_z, route_h = [], []

    def after(k):
        if k == 1:
            load_wo.wait()
            pl.semaphore_wait(barrier, len(peers))
            for dz in range(1, z_n):
                route_z.append(push(routes.at[0, 0, 0], routes.at[0, 0, dz], to_z(dz)))
            send_part([0, 1])
        elif k == h_n - 2:
            send_part([k])
            for c in route_z:
                c.wait_recv()
            for j in range(1, h_n):
                route_h.append(
                    push(routes.at[0, 0], routes.at[0, j], to_yx(j // x_n, j % x_n))
                )

    load_k[0].wait()
    load_v[0].wait()
    steps = [(k, c) for k in range(reqs) for c in range(chunks)]
    ahead = score(0, 0)
    for i, (k, c) in enumerate(steps):
        now_s = ahead
        if c == chunks - 1 and k + 1 < reqs:
            load_k[k + 1].wait()
            load_v[k + 1].wait()
        if i + 1 < len(steps):
            ahead = score(*steps[i + 1])
        if c == 0:
            admitted = jnp.concatenate([closed[which[k]]] * groups, axis=0)
            st = jnp.where(admitted > 0.5, dot_nt(state[k], tk_ref[which[k]]), NEG)
            m = jnp.max(st, -1, keepdims=True)
            p = jnp.exp2(st - m)
            l = jnp.sum(p, -1, keepdims=True)
            acc = dot_nn(p.astype(BF16), tv_ref[which[k]])
        now = jnp.maximum(m, jnp.max(now_s, -1, keepdims=True))
        p = jnp.exp2(now_s - now)
        fade = jnp.exp2(m - now)
        l = l * fade + jnp.sum(p, -1, keepdims=True)
        acc = acc * fade + dot_nn(p.astype(BF16), vbuf[k % 2, c * CHUNK : (c + 1) * CHUNK])
        m = now
        if c == chunks - 1:
            o = (acc / l).astype(BF16)
            for g in range(groups):
                attended[k, :, g * hd : (g + 1) * hd] = o[g * tree : (g + 1) * tree]
            if k + 2 < reqs:
                load_k[k + 2].start()
                load_v[k + 2].start()
            after(k)

    resid = hid_ref[...].astype(F32) + project([reqs - 1])
    load_dn.start()
    for k in range(h_n - 1):
        arrivals[k].wait_recv()
        resid = resid + head_in[k].astype(F32)
    resid_ref[...] = resid
    normed = (
        resid * lax.rsqrt(jnp.mean(resid * resid, -1, keepdims=True) + 1e-06) * gain_ref[...]
    ).astype(BF16)
    for f in range(2):
        bank[0, f, 0, 0, 0] = normed[:, f * half : (f + 1) * half]
    got = {}

    def gather(f, dz, dy, dx, src, peer):
        got[f, dz, dy, dx] = push(
            bank.at[(0, f, dz) + src], bank.at[0, f, dz, dy, dx], peer
        )

    for dz in range(1, z_n):
        for f in range(2):
            got[f, dz, 0, 0] = push(bank.at[0, f, 0, 0, 0], bank.at[0, f, dz, 0, 0], to_z(dz))

    crossed = {}

    def cross(f, dz, dy, dx):
        crossed[f, dz, dy, dx] = push(
            bank.at[0, f, dz, dy, dx], bank.at[1, f, dz, dy, dx], partner
        )

    def stage_a(dz):
        for f in range(2):
            if dz:
                got[f, dz, 0, 0].wait_recv()
            cross(f, dz, 0, 0)
            for dx in range(1, x_n):
                gather(f, dz, 0, dx, (0, 0), to_yx(0, dx)) if f == 0 else None
            for dy in range(1, y_n):
                gather(f, dz, dy, 0, (0, 0), to_yx(dy, 0)) if f == 1 else None
        for dy in range(1, y_n):
            gather(0, dz, dy, 0, (0, 0), to_yx(dy, 0))
        for dx in range(1, x_n):
            gather(1, dz, 0, dx, (0, 0), to_yx(0, dx))

    def stage_b(dz):
        for dx in range(1, x_n):
            got[0, dz, 0, dx].wait_recv()
            for dy in range(1, y_n):
                gather(0, dz, dy, dx, (0, dx), to_yx(dy, 0))
            cross(0, dz, 0, dx)
        for dy in range(1, y_n):
            got[1, dz, dy, 0].wait_recv()
            for dx in range(1, x_n):
                gather(1, dz, dy, dx, (dy, 0), to_yx(0, dx))
            cross(1, dz, dy, 0)

    def stage_c(dz):
        for f in range(2):
            for dy in range(y_n):
                for dx in range(x_n):
                    seen = (dy == 0 and dx == 0) or (f == 0 and dy == 0) or (f == 1 and dx == 0)
                    if not seen:
                        got[f, dz, dy, dx].wait_recv()
                        cross(f, dz, dy, dx)

    count = 2 * h_n * tok
    apart = 1 if h_n * tok <= 128 else y_n

    def experts(dz):
        for f in range(2):
            for dy in range(y_n):
                for dx in range(x_n):
                    crossed[f, dz, dy, dx].wait_recv()
        pick = lax.broadcasted_iota(jnp.int32, (1, lanes), 1) == mine
        for part in range(apart):
            ys = slice(part * (y_n // apart), (part + 1) * (y_n // apart))
            left = bank[:, 0, dz, ys].reshape(count // apart, half)
            right = bank[:, 1, dz, ys].reshape(count // apart, half)
            hs = slice(ys.start * x_n, ys.stop * x_n)
            named = routes[:, hs, dz].reshape(count // apart, lanes)
            weight = jnp.sum(jnp.where(pick, named, 0.0), -1, keepdims=True)
            mixed = dot_nn(left, gu[:half]) + dot_nn(right, gu[half:])
            hidden = mixed.shape[1] // 2
            gate = mixed[:, :hidden]
            active = (gate / (1.0 + jnp.exp(-gate)) * mixed[:, hidden:]).astype(BF16)
            result = jnp.where(weight > 0.0, dot_nn(active, wide[:ffe]) * weight, 0.0).astype(BF16)
            shaped = result.reshape(2, y_n // apart, x_n, tok, model)
            for f in range(2):
                sums[f, dz, ys] = shaped[0, ..., f * half : (f + 1) * half]
                bank[1, f, dz, ys] = shaped[1, ..., f * half : (f + 1) * half]

    paired, firsts, seconds, ends = {}, {}, {}, {}

    def back_pair(dz):
        for f in range(2):
            paired[f, dz] = push(
                bank.at[1, f, dz], pair_in.at[f, dz], partner
            )

    def back_first(dz):
        for f in range(2):
            paired[f, dz].wait_recv()
            sums[f, dz] = (sums[f, dz].astype(F32) + pair_in[f, dz].astype(F32)).astype(BF16)
            if f == 0:
                for dy in range(1, y_n):
                    firsts[f, dz, dy] = push(
                        sums.at[f, dz, dy], first_in.at[f, dz, dy - 1], to_yx(y_n - dy, 0)
                    )
            else:
                for dx in range(1, x_n):
                    firsts[f, dz, dx] = push(
                        sums.at[f, dz, :, dx], first_in.at[f, dz, dx - 1], to_yx(0, x_n - dx)
                    )

    def back_second(dz):
        for f in range(2):
            total = sums[f, dz, 0] if f == 0 else sums[f, dz, :, 0]
            total = total.astype(F32)
            for d in range(1, y_n if f == 0 else x_n):
                firsts[f, dz, d].wait_recv()
                total = total + first_in[f, dz, d - 1].astype(F32)
            if f == 0:
                sums[f, dz, 0] = total.astype(BF16)
                for dx in range(1, x_n):
                    seconds[f, dz, dx] = push(
                        sums.at[f, dz, 0, dx], second_in.at[f, dz, dx - 1], to_yx(0, x_n - dx)
                    )
            else:
                sums[f, dz, :, 0] = total.astype(BF16)
                for dy in range(1, y_n):
                    seconds[f, dz, dy] = push(
                        sums.at[f, dz, dy, 0], second_in.at[f, dz, dy - 1], to_yx(y_n - dy, 0)
                    )

    def back_end(dz):
        for f in range(2):
            total = sums[f, dz, 0, 0].astype(F32)
            for d in range(1, x_n if f == 0 else y_n):
                seconds[f, dz, d].wait_recv()
                total = total + second_in[f, dz, d - 1].astype(F32)
            if dz:
                sums[f, dz, 0, 0] = total.astype(BF16)
                ends[f, dz] = push(sums.at[f, dz, 0, 0], z_in.at[f, dz - 1], to_z(z_n - dz))
            else:
                cols = slice(f * half, (f + 1) * half)
                resid_ref[:, cols] = resid_ref[:, cols] + total

    order = list(range(1, z_n)) + [0]

    def back(j):
        for stage, lag in ((back_end, 3), (back_second, 2), (back_first, 1)):
            if 0 <= j - lag < z_n:
                stage(order[j - lag])

    ran = 0
    for i in range(z_n + 2):
        for stage, lag in ((stage_a, 0), (stage_b, 1), (stage_c, 2)):
            if 0 <= i - lag < z_n:
                stage(i - lag)
        if i == 1:
            for c in route_h:
                c.wait_recv()
            crossed_routes = push(routes.at[0], routes.at[1], partner)
        if i == 2:
            load_gu.wait()
            load_dn.wait()
            crossed_routes.wait_recv()
        while ran < z_n and (i == z_n + 1 or order[ran] <= i - 2 and order[ran] > 0):
            experts(order[ran])
            back_pair(order[ran])
            back(ran)
            ran += 1
    for j in range(z_n, z_n + 3):
        back(j)
    for f in range(2):
        cols = slice(f * half, (f + 1) * half)
        total = resid_ref[:, cols]
        for dz in range(1, z_n):
            ends[f, dz].wait_recv()
            total = total + z_in[f, dz - 1].astype(F32)
        out_ref[:, cols] = total.astype(BF16)
    for c in made:
        c.wait_send()
    assert len(made) == copy_count(*dims)


def layer(dims, q, tk, tv, ck, cv, lengths, parents, out_weight, hidden, gain, ids, route, gate_up,
          down):
    z_n, y_n, x_n = dims
    tok, model = hidden.shape
    half = model // 2
    h_n = y_n * x_n
    reqs, tree, width = q.shape
    cache, hd = ck.shape[2:]
    experts = gate_up.shape[0] * 2 * z_n * h_n
    assert gate_up.shape[0] == 1 and ck.shape[1] == 1
    lanes = -(-experts // LANES) * LANES
    most = max(y_n, x_n)
    copies = copy_count(*dims)
    vmem = pl.BlockSpec(memory_space=pltpu.VMEM)
    return pl.pallas_call(
        functools.partial(layer_kernel, dims),
        out_shape=jax.ShapeDtypeStruct((tok, model), BF16),
        in_specs=[pl.BlockSpec(memory_space=pltpu.SMEM)] + [vmem] * 8
        + [pl.BlockSpec(memory_space=pl.ANY)] * 5,
        out_specs=vmem,
        scratch_shapes=[
            pltpu.VMEM((2, cache, hd), BF16),
            pltpu.VMEM((2, cache, hd), BF16),
            pltpu.VMEM((max(width, down.shape[1]), model), BF16),
            pltpu.VMEM((reqs, tree, tree), F32),
            pltpu.VMEM((reqs, tree, width), BF16),
            pltpu.VMEM((h_n - 1, tok, model), BF16),
            pltpu.VMEM((h_n - 1, tok, model), BF16),
            pltpu.VMEM((2, h_n, z_n, tok, lanes), F32),
            pltpu.VMEM((2, 2, z_n, y_n, x_n, tok, half), BF16),
            pltpu.VMEM((2, z_n, y_n, x_n, tok, half), BF16),
            pltpu.VMEM((2, z_n, y_n, x_n, tok, half), BF16),
            pltpu.VMEM((2, z_n, most - 1, most, tok, half), BF16),
            pltpu.VMEM((2, z_n, most - 1, tok, half), BF16),
            pltpu.VMEM((2, z_n - 1, tok, half), BF16),
            pltpu.VMEM((tok, model), F32),
            pltpu.VMEM(gate_up.shape[1:], BF16),
            pltpu.SemaphoreType.DMA((copies,)),
            pltpu.SemaphoreType.DMA((copies,)),
            pltpu.SemaphoreType.DMA((3,)),
            pltpu.SemaphoreType.DMA((2, reqs)),
        ],
        compiler_params=pltpu.CompilerParams(
            collective_id=0, has_side_effects=True, vmem_limit_bytes=67043328
        ),
    )(lengths, q, tk, tv, parents, hidden, gain.reshape(1, -1), ids.T, route.T, ck, cv,
      out_weight, gate_up, down)


def per_device(
    dims, queries, tree_keys, tree_values, cache_keys, cache_values, cache_lengths, tree_parents,
    out_weight, hidden, norm_gain, expert_ids, route_weights, expert_gate_up, expert_down,
):
    return layer(
        dims, queries, tree_keys, tree_values, cache_keys, cache_values, cache_lengths,
        tree_parents, out_weight, hidden, norm_gain, expert_ids, route_weights, expert_gate_up,
        expert_down,
    )


def solution(mesh):
    heads = mesh.shape["head"]
    x_n = math.isqrt(heads)
    while heads % x_n:
        x_n -= 1
    assert mesh.shape["sec"] == 2
    dims = (mesh.shape["req"], heads // x_n, x_n)
    tokens = ("sec", "req", "head")
    in_specs = (
        P(("sec", "req"), None, "head"),
        P(("sec", "req"), None, "head"),
        P(("sec", "req"), None, "head"),
        P(("sec", "req"), "head", None, None),
        P(("sec", "req"), "head", None, None),
        P(("sec", "req")),
        P(("sec", "req"), None),
        P("head", None),
        P(tokens, None),
        P(),
        P(tokens, None),
        P(tokens, None),
        P(tokens, None, None),
        P(tokens, None, None),
    )
    return jax.shard_map(
        functools.partial(per_device, dims), mesh=mesh, in_specs=in_specs,
        out_specs=P(tokens, None), check_vma=False,
    )
```

time: 92.1 us -> 77.7 us (0.84)
  Pallas kernels: 90.3 us -> 76 us
    pallas_call x2 -> x1, Pallas kernels: 90.3 us -> 76 us  [layer(): pl.pallas_call(functools.partial(layer_kernel, dims), out_shape=jax.Shape...]
where the time goes in v1:
time: 77.7 us; the launch traced here: 77.5 us
  Pallas kernels  76 us (98%)
  local copies, waits for them, and re-layouts  1.57 us (2%)
    pallas_call x1, Pallas kernels, layer(): pl.pallas_call(functools.partial(layer_kernel, dims), out_shape=jax.Shape...  76 us
    unnamed x1, local copies, waits for them, and re-layouts  1.57 us

profile of v1, /device:TPU:0, one launch (start us, length us, event | category | flops | bytes accessed | tf_op | source)
XLA Modules:
  0.0 77.5 jit_solution(16592033484183616746)
XLA Ops:
  0.0 76.0 %shard_map.136 = bf16[32,2048]{1,0:T(8,128)(2,1)} custom-call(s32[4]{0:T(128)} %len_ref.1, bf16[4,32,1024]{2,1,0:T(8,128)(2,1)} %q_ref.1, bf16[4,32,128]{2,1,0:T(8,128)(2,1)} %tk_ref.1, bf16[4,32,128]{2,1,0:T(8,128)(2,1)} %tv_ref.1, s32[4,32]{1,0:T(4,128)} %par_ref.1, bf16[32,2048]{1,0:T(8,128)(2,1)} %hid_ref.1, f32[1,2048]{1,0:T(1,128)} %bitcast.3, ...), custom_call_target="tpu_custom_call" | custom-call | tf_op jit(solution)/shard_map/pallas_call | solution.py:408
  76.0 1.6 %copy.16 = bf16[32,2048]{1,0:T(8,128)(2,1)} copy(bf16[32,2048]{1,0:T(8,128)(2,1)} %shard_map.136) | data formatting | bytes 262144

commit v2 on v1

--- a/solution.py
+++ b/solution.py
@@ -49,7 +49,7 @@
     dims, len_ref, q_ref, tk_ref, tv_ref, par_ref, hid_ref, gain_ref, ids_ref, rw_ref,
     ck_hbm, cv_hbm, wo_hbm, gu_hbm, dn_hbm, out_ref,
     kbuf, vbuf, wide, closed, attended, part_out, head_in, routes,
-    bank, sums, pair_in, first_in, second_in, z_in, resid_ref, gu,
+    bank, active, sums, pair_in, first_in, second_in, z_in, resid_ref, gu,
     send, recv, load_sem, kv_sem,
 ):
     z_n, y_n, x_n = dims
@@ -66,8 +66,12 @@
     def to_head(k):
         return {"head": lax.rem(h + k, h_n)}
 
-    def to_z(k):
-        return {"req": lax.rem(z + k, z_n)}
+    def to_z(d):
+        other = z
+        for bit in range(z_n.bit_length()):
+            if d >> bit & 1:
+                other = other + 2**bit - 2 ** (bit + 1) * lax.rem(z // 2**bit, 2)
+        return {"req": other}
 
     def to_yx(dy, dx):
         return {"head": lax.rem(y + dy, y_n) * x_n + lax.rem(x + dx, x_n)}
@@ -81,7 +85,7 @@
         )
 
     reqs, tree, width = q_ref.shape
-    assert reqs == h_n and tree == tok
+    assert reqs == h_n and tree == tok and z_n & (z_n - 1) == 0
     which = [lax.rem(h + k, h_n) for k in range(1, h_n + 1)]
     load_k = [
         pltpu.make_async_copy(ck_hbm.at[which[k], 0], kbuf.at[k % 2], kv_sem.at[0, k])
@@ -95,11 +99,8 @@
     load_gu = pltpu.make_async_copy(gu_hbm.at[0], gu, load_sem.at[0])
     ffe = dn_hbm.shape[1]
     load_dn = pltpu.make_async_copy(dn_hbm.at[0], wide.at[pl.ds(0, ffe)], load_sem.at[1])
-    for k in range(2):
-        load_k[k].start()
-        load_v[k].start()
-    load_wo.start()
-    load_gu.start()
+    load_k[0].start()
+    load_v[0].start()
 
     made = []
 
@@ -155,26 +156,34 @@
         for k in ks:
             arrivals.append(push(part_out.at[k], head_in.at[k], to_head(k + 1)))
 
-    route_z, route_h = [], []
+    route_z, route_h, route_s = [], [], []
 
     def after(k):
-        if k == 1:
-            load_wo.wait()
-            pl.semaphore_wait(barrier, len(peers))
-            for dz in range(1, z_n):
-                route_z.append(push(routes.at[0, 0, 0], routes.at[0, 0, dz], to_z(dz)))
-            send_part([0, 1])
-        elif k == h_n - 2:
-            send_part([k])
+        if k == 0:
             for c in route_z:
                 c.wait_recv()
             for j in range(1, h_n):
                 route_h.append(
                     push(routes.at[0, 0], routes.at[0, j], to_yx(j // x_n, j % x_n))
                 )
-
+        elif k == 1:
+            load_wo.wait()
+            load_gu.start()
+            send_part([0, 1])
+        elif k == h_n - 2:
+            send_part([k])
+            for c in route_h:
+                c.wait_recv()
+            route_s.append(push(routes.at[0], routes.at[1], partner))
+
+    pl.semaphore_wait(barrier, len(peers))
+    for d in range(1, z_n):
+        route_z.append(push(routes.at[0, 0, 0], routes.at[0, 0, d], to_z(d)))
     load_k[0].wait()
     load_v[0].wait()
+    load_k[1].start()
+    load_v[1].start()
+    load_wo.start()
     steps = [(k, c) for k in range(reqs) for c in range(chunks)]
     ahead = score(0, 0)
     for i, (k, c) in enumerate(steps):
@@ -217,174 +226,165 @@
     ).astype(BF16)
     for f in range(2):
         bank[0, f, 0, 0, 0] = normed[:, f * half : (f + 1) * half]
-    got = {}
-
-    def gather(f, dz, dy, dx, src, peer):
-        got[f, dz, dy, dx] = push(
-            bank.at[(0, f, dz) + src], bank.at[0, f, dz, dy, dx], peer
+    got, crossed = {}, {}
+
+    def gather(f, d, dy, dx, src, peer):
+        got[f, d, dy, dx] = push(bank.at[(0, f, d) + src], bank.at[0, f, d, dy, dx], peer)
+
+    def cross(f, d, dy, dx):
+        crossed[f, d, dy, dx] = push(
+            bank.at[0, f, d, dy, dx], bank.at[1, f, d, dy, dx], partner
         )
 
-    for dz in range(1, z_n):
-        for f in range(2):
-            got[f, dz, 0, 0] = push(bank.at[0, f, 0, 0, 0], bank.at[0, f, dz, 0, 0], to_z(dz))
-
-    crossed = {}
-
-    def cross(f, dz, dy, dx):
-        crossed[f, dz, dy, dx] = push(
-            bank.at[0, f, dz, dy, dx], bank.at[1, f, dz, dy, dx], partner
-        )
-
-    def stage_a(dz):
-        for f in range(2):
-            if dz:
-                got[f, dz, 0, 0].wait_recv()
-            cross(f, dz, 0, 0)
+    def stage_a(d):
+        if d:
+            for f in range(2):
+                got[f, d, 0, 0].wait_recv()
+                for low in [2**b for b in range((d & -d).bit_length() - 1)]:
+                    got[f, d + low, 0, 0] = push(
+                        bank.at[0, f, d, 0, 0], bank.at[0, f, d + low, 0, 0], to_z(low)
+                    )
+        for dx in range(1, x_n):
+            gather(0, d, 0, dx, (0, 0), to_yx(0, dx))
+        for dy in range(1, y_n):
+            gather(1, d, dy, 0, (0, 0), to_yx(dy, 0))
+        for dy in range(1, y_n):
+            gather(0, d, dy, 0, (0, 0), to_yx(dy, 0))
+        for dx in range(1, x_n):
+            gather(1, d, 0, dx, (0, 0), to_yx(0, dx))
+        for f in range(2):
+            cross(f, d, 0, 0)
+
+    def stage_b(d):
+        for dx in range(1, x_n):
+            got[0, d, 0, dx].wait_recv()
+            for dy in range(1, y_n):
+                gather(0, d, dy, dx, (0, dx), to_yx(dy, 0))
+        for dy in range(1, y_n):
+            got[1, d, dy, 0].wait_recv()
             for dx in range(1, x_n):
-                gather(f, dz, 0, dx, (0, 0), to_yx(0, dx)) if f == 0 else None
-            for dy in range(1, y_n):
-                gather(f, dz, dy, 0, (0, 0), to_yx(dy, 0)) if f == 1 else None
+                gather(1, d, dy, dx, (dy, 0), to_yx(0, dx))
+        for dx in range(1, x_n):
+            cross(0, d, 0, dx)
         for dy in range(1, y_n):
-            gather(0, dz, dy, 0, (0, 0), to_yx(dy, 0))
-        for dx in range(1, x_n):
-            gather(1, dz, 0, dx, (0, 0), to_yx(0, dx))
-
-    def stage_b(dz):
-        for dx in range(1, x_n):
-            got[0, dz, 0, dx].wait_recv()
-            for dy in range(1, y_n):
-                gather(0, dz, dy, dx, (0, dx), to_yx(dy, 0))
-            cross(0, dz, 0, dx)
-        for dy in range(1, y_n):
-            got[1, dz, dy, 0].wait_recv()
-            for dx in range(1, x_n):
-                gather(1, dz, dy, dx, (dy, 0), to_yx(0, dx))
-            cross(1, dz, dy, 0)
-
-    def stage_c(dz):
-        for f in range(2):
-            for dy in range(y_n):
-                for dx in range(x_n):
-                    seen = (dy == 0 and dx == 0) or (f == 0 and dy == 0) or (f == 1 and dx == 0)
-                    if not seen:
-                        got[f, dz, dy, dx].wait_recv()
-                        cross(f, dz, dy, dx)
-
-    count = 2 * h_n * tok
-    apart = 1 if h_n * tok <= 128 else y_n
-
-    def experts(dz):
-        for f in range(2):
-            for dy in range(y_n):
-                for dx in range(x_n):
-                    crossed[f, dz, dy, dx].wait_recv()
+            cross(1, d, dy, 0)
+
+    def stage_c(d):
+        late = [(0, dy, 0) for dy in range(1, y_n)] + [(1, 0, dx) for dx in range(1, x_n)]
+        late += [(f, dy, dx) for f in range(2) for dy in range(1, y_n) for dx in range(1, x_n)]
+        for f, dy, dx in late:
+            got[f, d, dy, dx].wait_recv()
+            cross(f, d, dy, dx)
+
+    rows = 2 * h_n * tok
+    hidden = gu.shape[1] // 2
+    step = hidden // 3
+    paired, firsts, seconds, ends = {}, {}, {}, {}
+
+    def compute(d, hooks):
+        for c in [crossed[f, d, dy, dx] for f in range(2) for dy in range(y_n) for dx in range(x_n)]:
+            c.wait_recv()
+        left = bank[:, 0, d].reshape(rows, half)
+        right = bank[:, 1, d].reshape(rows, half)
+        for j in range(3):
+            cols = slice(j * step, (j + 1) * step)
+            ups = slice(hidden + j * step, hidden + (j + 1) * step)
+            gate = dot_nn(left, gu[:half, cols]) + dot_nn(right, gu[half:, cols])
+            up = dot_nn(left, gu[:half, ups]) + dot_nn(right, gu[half:, ups])
+            active[:, cols] = (gate / (1.0 + jnp.exp(-gate)) * up).astype(BF16)
+            hooks[j]()
         pick = lax.broadcasted_iota(jnp.int32, (1, lanes), 1) == mine
-        for part in range(apart):
-            ys = slice(part * (y_n // apart), (part + 1) * (y_n // apart))
-            left = bank[:, 0, dz, ys].reshape(count // apart, half)
-            right = bank[:, 1, dz, ys].reshape(count // apart, half)
-            hs = slice(ys.start * x_n, ys.stop * x_n)
-            named = routes[:, hs, dz].reshape(count // apart, lanes)
-            weight = jnp.sum(jnp.where(pick, named, 0.0), -1, keepdims=True)
-            mixed = dot_nn(left, gu[:half]) + dot_nn(right, gu[half:])
-            hidden = mixed.shape[1] // 2
-            gate = mixed[:, :hidden]
-            active = (gate / (1.0 + jnp.exp(-gate)) * mixed[:, hidden:]).astype(BF16)
-            result = jnp.where(weight > 0.0, dot_nn(active, wide[:ffe]) * weight, 0.0).astype(BF16)
-            shaped = result.reshape(2, y_n // apart, x_n, tok, model)
-            for f in range(2):
-                sums[f, dz, ys] = shaped[0, ..., f * half : (f + 1) * half]
-                bank[1, f, dz, ys] = shaped[1, ..., f * half : (f + 1) * half]
-
-    paired, firsts, seconds, ends = {}, {}, {}, {}
-
-    def back_pair(dz):
-        for f in range(2):
-            paired[f, dz] = push(
-                bank.at[1, f, dz], pair_in.at[f, dz], partner
-            )
-
-    def back_first(dz):
-        for f in range(2):
-            paired[f, dz].wait_recv()
-            sums[f, dz] = (sums[f, dz].astype(F32) + pair_in[f, dz].astype(F32)).astype(BF16)
+        named = routes[:, :, d].reshape(rows, lanes)
+        weight = jnp.sum(jnp.where(pick, named, 0.0), -1, keepdims=True)
+        for f in range(2):
+            result = dot_nn(active[...], wide[:ffe, f * half : (f + 1) * half]) * weight
+            shaped = result.astype(BF16).reshape(2, y_n, x_n, tok, half)
+            sums[f, d] = shaped[0]
+            bank[1, f, d] = shaped[1]
+            paired[f, d] = push(bank.at[1, f, d], pair_in.at[f, d], partner)
+            hooks[3 + f]()
+
+    def back_first(d):
+        for f in range(2):
+            paired[f, d].wait_recv()
+            sums[f, d] = (sums[f, d].astype(F32) + pair_in[f, d].astype(F32)).astype(BF16)
             if f == 0:
                 for dy in range(1, y_n):
-                    firsts[f, dz, dy] = push(
-                        sums.at[f, dz, dy], first_in.at[f, dz, dy - 1], to_yx(y_n - dy, 0)
+                    firsts[f, d, dy] = push(
+                        sums.at[f, d, dy], first_in.at[f, d, dy - 1], to_yx(y_n - dy, 0)
                     )
             else:
                 for dx in range(1, x_n):
-                    firsts[f, dz, dx] = push(
-                        sums.at[f, dz, :, dx], first_in.at[f, dz, dx - 1], to_yx(0, x_n - dx)
+                    firsts[f, d, dx] = push(
+                        sums.at[f, d, :, dx], first_in.at[f, d, dx - 1], to_yx(0, x_n - dx)
                     )
 
-    def back_second(dz):
-        for f in range(2):
-            total = sums[f, dz, 0] if f == 0 else sums[f, dz, :, 0]
+    def back_second(d):
+        for f in range(2):
+            total = sums[f, d, 0] if f == 0 else sums[f, d, :, 0]
             total = total.astype(F32)
-            for d in range(1, y_n if f == 0 else x_n):
-                firsts[f, dz, d].wait_recv()
-                total = total + first_in[f, dz, d - 1].astype(F32)
+            for k in range(1, y_n if f == 0 else x_n):
+                firsts[f, d, k].wait_recv()
+                total = total + first_in[f, d, k - 1].astype(F32)
             if f == 0:
-                sums[f, dz, 0] = total.astype(BF16)
+                sums[f, d, 0] = total.astype(BF16)
                 for dx in range(1, x_n):
-                    seconds[f, dz, dx] = push(
-                        sums.at[f, dz, 0, dx], second_in.at[f, dz, dx - 1], to_yx(0, x_n - dx)
+                    seconds[f, d, dx] = push(
+                        sums.at[f, d, 0, dx], second_in.at[f, d, dx - 1], to_yx(0, x_n - dx)
                     )
             else:
-                sums[f, dz, :, 0] = total.astype(BF16)
+                sums[f, d, :, 0] = total.astype(BF16)
                 for dy in range(1, y_n):
-                    seconds[f, dz, dy] = push(
-                        sums.at[f, dz, dy, 0], second_in.at[f, dz, dy - 1], to_yx(y_n - dy, 0)
+                    seconds[f, d, dy] = push(
+                        sums.at[f, d, dy, 0], second_in.at[f, d, dy - 1], to_yx(y_n - dy, 0)
                     )
 
-    def back_end(dz):
-        for f in range(2):
-            total = sums[f, dz, 0, 0].astype(F32)
-            for d in range(1, x_n if f == 0 else y_n):
-                seconds[f, dz, d].wait_recv()
-                total = total + second_in[f, dz, d - 1].astype(F32)
-            if dz:
-                sums[f, dz, 0, 0] = total.astype(BF16)
-                ends[f, dz] = push(sums.at[f, dz, 0, 0], z_in.at[f, dz - 1], to_z(z_n - dz))
+    def back_end(d):
+        for f in range(2):
+            total = sums[f, d, 0, 0].astype(F32)
+            for k in range(1, x_n if f == 0 else y_n):
+                seconds[f, d, k].wait_recv()
+                total = total + second_in[f, d, k - 1].astype(F32)
+            if d:
+                sums[f, d, 0, 0] = total.astype(BF16)
+                ends[f, d] = push(sums.at[f, d, 0, 0], z_in.at[f, d - 1], to_z(d))
             else:
                 cols = slice(f * half, (f + 1) * half)
                 resid_ref[:, cols] = resid_ref[:, cols] + total
 
-    order = list(range(1, z_n)) + [0]
-
-    def back(j):
-        for stage, lag in ((back_end, 3), (back_second, 2), (back_first, 1)):
-            if 0 <= j - lag < z_n:
-                stage(order[j - lag])
-
-    ran = 0
-    for i in range(z_n + 2):
-        for stage, lag in ((stage_a, 0), (stage_b, 1), (stage_c, 2)):
-            if 0 <= i - lag < z_n:
-                stage(i - lag)
-        if i == 1:
-            for c in route_h:
-                c.wait_recv()
-            crossed_routes = push(routes.at[0], routes.at[1], partner)
-        if i == 2:
-            load_gu.wait()
-            load_dn.wait()
-            crossed_routes.wait_recv()
-        while ran < z_n and (i == z_n + 1 or order[ran] <= i - 2 and order[ran] > 0):
-            experts(order[ran])
-            back_pair(order[ran])
-            back(ran)
-            ran += 1
-    for j in range(z_n, z_n + 3):
-        back(j)
+    done = set()
+
+    def run(*stages):
+        for stage, d in stages:
+            if 0 <= d < z_n and (stage, d) not in done:
+                done.add((stage, d))
+                stage(d)
+
+    for d in [2**b for b in range(z_n.bit_length() - 1)]:
+        for f in range(2):
+            got[f, d, 0, 0] = push(bank.at[0, f, 0, 0, 0], bank.at[0, f, d, 0, 0], to_z(d))
+    run((stage_a, 0), (stage_b, 0), (stage_a, 1))
+    run((stage_c, 0))
+    load_gu.wait()
+    load_dn.wait()
+    route_s[0].wait_recv()
+    n = z_n - 1
+    for i in range(z_n):
+        compute(i, [
+            lambda: run((stage_b, i + 1)),
+            lambda: run((back_first, i - 1 or -1)),
+            lambda: run((stage_a, i + 2)),
+            lambda: run((back_second, i - 2 or -1)),
+            lambda: run((stage_c, i + 1), (back_end, i - 3 or -1)),
+        ])
+    run((back_first, n), (back_end, n - 2), (back_second, n - 1), (back_second, n))
+    run((back_first, 0), (back_end, n - 1), (back_end, n), (back_second, 0), (back_end, 0))
     for f in range(2):
         cols = slice(f * half, (f + 1) * half)
         total = resid_ref[:, cols]
-        for dz in range(1, z_n):
-            ends[f, dz].wait_recv()
-            total = total + z_in[f, dz - 1].astype(F32)
+        for d in range(1, z_n):
+            ends[f, d].wait_recv()
+            total = total + z_in[f, d - 1].astype(F32)
         out_ref[:, cols] = total.astype(BF16)
     for c in made:
         c.wait_send()
@@ -421,6 +421,7 @@
             pltpu.VMEM((h_n - 1, tok, model), BF16),
             pltpu.VMEM((2, h_n, z_n, tok, lanes), F32),
             pltpu.VMEM((2, 2, z_n, y_n, x_n, tok, half), BF16),
+            pltpu.VMEM((2 * h_n * tok, down.shape[1]), BF16),
             pltpu.VMEM((2, z_n, y_n, x_n, tok, half), BF16),
             pltpu.VMEM((2, z_n, y_n, x_n, tok, half), BF16),
             pltpu.VMEM((2, z_n, most - 1, most, tok, half), BF16),

time: 77.7 us -> 72.9 us (0.938)
  Pallas kernels: 76 us -> 71.2 us
    pallas_call x1, Pallas kernels: 76 us -> 71.2 us  [layer(): pl.pallas_call(functools.partial(layer_kernel, dims), out_shape=jax.Shape...]
where the time goes in v2:
time: 72.9 us; the launch traced here: 72.8 us
  Pallas kernels  71.2 us (98%)
  local copies, waits for them, and re-layouts  1.57 us (2%)
    pallas_call x1, Pallas kernels, layer(): pl.pallas_call(functools.partial(layer_kernel, dims), out_shape=jax.Shape...  71.2 us
    unnamed x1, local copies, waits for them, and re-layouts  1.57 us

profile of v2, /device:TPU:0, one launch (start us, length us, event | category | flops | bytes accessed | tf_op | source)
XLA Modules:
  0.0 72.8 jit_solution(7938885402411285182)
XLA Ops:
  0.0 71.2 %shard_map.136 = bf16[32,2048]{1,0:T(8,128)(2,1)} custom-call(s32[4]{0:T(128)} %len_ref.1, bf16[4,32,1024]{2,1,0:T(8,128)(2,1)} %q_ref.1, bf16[4,32,128]{2,1,0:T(8,128)(2,1)} %tk_ref.1, bf16[4,32,128]{2,1,0:T(8,128)(2,1)} %tv_ref.1, s32[4,32]{1,0:T(4,128)} %par_ref.1, bf16[32,2048]{1,0:T(8,128)(2,1)} %hid_ref.1, f32[1,2048]{1,0:T(1,128)} %bitcast.3, ...), custom_call_target="tpu_custom_call" | custom-call | tf_op jit(solution)/shard_map/pallas_call | solution.py:408
  71.2 1.6 %copy.16 = bf16[32,2048]{1,0:T(8,128)(2,1)} copy(bf16[32,2048]{1,0:T(8,128)(2,1)} %shard_map.136) | data formatting | bytes 262144

commit v3 on v2

--- a/solution.py
+++ b/solution.py
@@ -11,7 +11,7 @@
 F32 = jnp.float32
 BF16 = jnp.bfloat16
 NEG = -1e30
-CHUNK = 2048
+CHUNK = 1024
 LANES = 128
 
 
@@ -86,7 +86,8 @@
 
     reqs, tree, width = q_ref.shape
     assert reqs == h_n and tree == tok and z_n & (z_n - 1) == 0
-    which = [lax.rem(h + k, h_n) for k in range(1, h_n + 1)]
+    away = [divmod(k, x_n) for k in reversed(range(h_n))]
+    which = [to_yx(*a)["head"] for a in away]
     load_k = [
         pltpu.make_async_copy(ck_hbm.at[which[k], 0], kbuf.at[k % 2], kv_sem.at[0, k])
         for k in range(reqs)
@@ -154,7 +155,7 @@
         for i, k in enumerate(ks):
             part_out[k] = out[i * tok : (i + 1) * tok]
         for k in ks:
-            arrivals.append(push(part_out.at[k], head_in.at[k], to_head(k + 1)))
+            arrivals.append(push(part_out.at[k], head_in.at[k], to_yx(*away[k])))
 
     route_z, route_h, route_s = [], [], []
 
@@ -363,8 +364,7 @@
     for d in [2**b for b in range(z_n.bit_length() - 1)]:
         for f in range(2):
             got[f, d, 0, 0] = push(bank.at[0, f, 0, 0, 0], bank.at[0, f, d, 0, 0], to_z(d))
-    run((stage_a, 0), (stage_b, 0), (stage_a, 1))
-    run((stage_c, 0))
+    run((stage_a, 0), (stage_b, 0), (stage_a, 1), (stage_c, 0), (stage_a, 2))
     load_gu.wait()
     load_dn.wait()
     route_s[0].wait_recv()
@@ -373,8 +373,8 @@
         compute(i, [
             lambda: run((stage_b, i + 1)),
             lambda: run((back_first, i - 1 or -1)),
-            lambda: run((stage_a, i + 2)),
-            lambda: run((back_second, i - 2 or -1)),
+            lambda: run((stage_a, i + 3)),
+            lambda: run((stage_b, i + 2), (back_second, i - 2 or -1)),
             lambda: run((stage_c, i + 1), (back_end, i - 3 or -1)),
         ])
     run((back_first, n), (back_end, n - 2), (back_second, n - 1), (back_second, n))

time: 72.9 us -> 72.9 us (level)
  no operation moved by 1% of the time
where the time goes in v3:
time: 72.9 us; the launch traced here: 72.8 us
  Pallas kernels  71.2 us (98%)
  local copies, waits for them, and re-layouts  1.57 us (2%)
    pallas_call x1, Pallas kernels, layer(): pl.pallas_call(functools.partial(layer_kernel, dims), out_shape=jax.Shape...  71.2 us
    unnamed x1, local copies, waits for them, and re-layouts  1.57 us

profile of v3, /device:TPU:0, one launch (start us, length us, event | category | flops | bytes accessed | tf_op | source)
XLA Modules:
  0.0 72.8 jit_solution(8043076874999384063)
XLA Ops:
  0.0 71.2 %shard_map.136 = bf16[32,2048]{1,0:T(8,128)(2,1)} custom-call(s32[4]{0:T(128)} %len_ref.1, bf16[4,32,1024]{2,1,0:T(8,128)(2,1)} %q_ref.1, bf16[4,32,128]{2,1,0:T(8,128)(2,1)} %tk_ref.1, bf16[4,32,128]{2,1,0:T(8,128)(2,1)} %tv_ref.1, s32[4,32]{1,0:T(4,128)} %par_ref.1, bf16[32,2048]{1,0:T(8,128)(2,1)} %hid_ref.1, f32[1,2048]{1,0:T(1,128)} %bitcast.3, ...), custom_call_target="tpu_custom_call" | custom-call | tf_op jit(solution)/shard_map/pallas_call | solution.py:408
  71.2 1.6 %copy.16 = bf16[32,2048]{1,0:T(8,128)(2,1)} copy(bf16[32,2048]{1,0:T(8,128)(2,1)} %shard_map.136) | data formatting | bytes 262144
